TPU v7x, 256 devices: a whole 4x4x8 slice. The times are simulated.
256 devices in a mesh: dp: 16 (over z, y_lo), dep: 4 (over x), hgt: 4 (over y_hi, core).
Axes of the slice: x: 4, y: 4 (y_hi: 2, y_lo: 2; y = y_hi * 2 + y_lo), z: 8, core: 2. Of those that a mesh axis runs over, the one named last changes fastest.
Arguments:
- volume: bfloat16 [16, 32, 8, 32, 128], P('dp', None, 'dep', 'hgt'), may hold values from -6 to 6
- kernel_first: bfloat16 [27, 64, 32], replicated, may hold values from -0.21875 to 0.21875
- kernel_second: bfloat16 [27, 128, 64], replicated, may hold values from -0.15625 to 0.15625
- cotangent: bfloat16 [16, 128, 8, 32, 128], P('dp', None, 'dep', 'hgt'), may hold values from -0.01171875 to 0.01171875
Outputs:
- features: bfloat16 [16, 128, 8, 32, 128], P('dp', None, 'dep', 'hgt')
- grad_first: float32 [27, 64, 32], P(None, 'dp')
- grad_second: float32 [27, 128, 64], P(None, 'dp')
All inputs are finite; a program needn't handle non-finite values.
Results may differ from a plain program's by a relative error of at most 0.0049.
Values may be sent and summed in bfloat16 or wider, within the bound.
A program may use at most 64 MiB of HBM per device.

v0:
```python
import jax
import jax.numpy as jnp
from jax import lax
from jax.sharding import PartitionSpec as P

OFFSETS = [
    (first, second, third) for first in (-1, 0, 1) for second in (-1, 0, 1) for third in (-1, 0, 1)
]


def extended_2(x, sides, width):
    for axis, dim in sides:
        size, length = (lax.axis_size(axis), x.shape[dim])
        up = [(i, (i + 1) % size) for i in range(size - 1)]
        down = [(j, i) for i, j in up]
        last = lax.slice_in_dim(x, length - width, length, axis=dim)
        leading = lax.slice_in_dim(x, 0, width, axis=dim)
        before = lax.ppermute(last, axis, up)
        after = lax.ppermute(leading, axis, down)
        x = jnp.concatenate([before, x, after], axis=dim)
    return x


def widen(field):
    return jnp.pad(field, ((0, 0), (0, 0), (0, 0), (0, 0), (1, 1)))


def window(padded, shift_d, shift_h, shift_w, depth, height, width):
    return padded[
        :,
        :,
        1 + shift_d : 1 + shift_d + depth,
        1 + shift_h : 1 + shift_h + height,
        1 + shift_w : 1 + shift_w + width,
    ]


def convolve(extended, kernel, depth, height, width):
    padded = widen(extended)
    total = None
    for number, shift in enumerate(OFFSETS):
        piece = window(padded, shift[0], shift[1], shift[2], depth, height, width)
        term = jnp.einsum(
            "oi,bidhw->bodhw", kernel[number], piece, preferred_element_type=jnp.float32
        )
        total = term if total is None else total + term
    return total


def kernel_grad(upstream, extended, depth, height, width):
    padded = widen(extended)
    parts = []
    for shift in OFFSETS:
        piece = window(padded, shift[0], shift[1], shift[2], depth, height, width)
        parts.append(
            jnp.einsum("bodhw,bidhw->oi", upstream, piece, preferred_element_type=jnp.float32)
        )
    return jnp.stack(parts)


def per_device(volume, kernel_first, kernel_second, cotangent):
    depth, height, width = (volume.shape[2], volume.shape[3], volume.shape[4])
    vol_rim = extended_2(volume, (("dep", 2), ("hgt", 3)), 1)
    pre = convolve(vol_rim, kernel_first, depth, height, width)
    hidden = jax.nn.silu(pre).astype(jnp.bfloat16)
    hidden_rim = extended_2(hidden, (("dep", 2), ("hgt", 3)), 1)
    features = convolve(hidden_rim, kernel_second, depth, height, width).astype(jnp.bfloat16)
    cot_rim = extended_2(cotangent, (("dep", 2), ("hgt", 3)), 1)
    grad_second = kernel_grad(cotangent, hidden_rim, depth, height, width)
    padded_cot = widen(cot_rim)
    back = None
    for number, shift in enumerate(OFFSETS):
        piece = window(padded_cot, -shift[0], -shift[1], -shift[2], depth, height, width)
        term = jnp.einsum(
            "oi,bodhw->bidhw", kernel_second[number], piece, preferred_element_type=jnp.float32
        )
        back = term if back is None else back + term
    sigma = jax.nn.sigmoid(pre)
    delta = (back * (sigma * (1.0 + pre * (1.0 - sigma)))).astype(jnp.bfloat16)
    grad_first = kernel_grad(delta, vol_rim, depth, height, width)
    summed = lax.psum((grad_first, grad_second), ("dep", "hgt"))
    grad_first, grad_second = (
        lax.psum_scatter(summed[0], "dp", scatter_dimension=1, tiled=True),
        lax.psum_scatter(summed[1], "dp", scatter_dimension=1, tiled=True),
    )
    return (features, grad_first, grad_second)


def solution(mesh):
    placed = (P("dp", None, "dep", "hgt", None), P(), P(), P("dp", None, "dep", "hgt", None))
    return jax.shard_map(
        per_device,
        mesh=mesh,
        in_specs=placed,
        out_specs=(P("dp", None, "dep", "hgt", None), P(None, "dp", None), P(None, "dp", None)),
        check_vma=False,
    )
```

profile of v0, /device:TPU:8, one launch (start us, length us, event | category | flops | bytes accessed | tf_op | source)
XLA Modules:
  0.0 418.0 jit_solution(17139515704096667886)
XLA Ops:
  8.2 3.5 collective-permute-start
  14.4 4.6 %collective-permute-start.8 = (bf16[1,128,1,8,128]{4,1,3,2,0:T(8,128)(2,1)S(1)}, bf16[1,128,1,8,128]{4,1,3,2,0:T(8,128)(2,1)S(1)}, u32[]{:S(2)}, u32[]{:S(2)}) collective-permute-start(bf16[1,128,1,8,128]{4,1,3,2,0:T(8,128)(2,1)S(1)} %get-tuple-element.14), channel_id=1, source_target_pairs={{0,4},{4,8},{8,12},{1,5},{5,9},{9,13},{2,6},{6,10},{10,14},{3,7},{... | collective-permute-start | bytes 786440 | tf_op jit(solution)/shard_map/ppermute | solution.py:18
  23.3 4.0 collective-permute-done.3
  35.5 4.6 %collective-permute-start.4 = (bf16[1,64,1,8,128]{4,1,3,2,0:T(8,128)(2,1)S(1)}, bf16[1,64,1,8,128]{4,1,3,2,0:T(8,128)(2,1)S(1)}, u32[]{:S(2)}, u32[]{:S(2)}) collective-permute-start(bf16[1,64,1,8,128]{4,1,3,2,0:T(8,128)(2,1)S(1)} %get-tuple-element.19), channel_id=1, source_target_pairs={{0,4},{4,8},{8,12},{1,5},{5,9},{9,13},{2,6},{6,10},{10,14},{3,7},{... | collective-permute-start | bytes 393224 | tf_op jit(solution)/shard_map/ppermute | solution.py:18
  42.6 4.4 %collective-permute-done.5 = bf16[1,64,1,8,128]{4,1,3,2,0:T(8,128)(2,1)S(1)} collective-permute-done((bf16[1,64,1,8,128]{4,1,3,2,0:T(8,128)(2,1)S(1)}, bf16[1,64,1,8,128]{4,1,3,2,0:T(8,128)(2,1)S(1)}, u32[]{:S(2)}, u32[]{:S(2)}) %collective-permute-start.5) | collective-permute-done | bytes 131104 | tf_op jit(solution)/shard_map/ppermute | solution.py:19
  47.0 4.6 %collective-permute-start.6 = (bf16[1,64,4,1,128]{4,1,3,2,0:T(8,128)(2,1)S(1)}, bf16[1,64,4,1,128]{4,1,3,2,0:T(8,128)(2,1)S(1)}, u32[]{:S(2)}, u32[]{:S(2)}) collective-permute-start(bf16[1,64,4,1,128]{4,1,3,2,0:T(8,128)(2,1)S(1)} %get-tuple-element.17), channel_id=1, source_target_pairs={{0,1},{1,2},{2,3},{4,5},{5,6},{6,7},{8,9},{9,10},{10,11},{12,13},{... | collective-permute-start | bytes 196616 | tf_op jit(solution)/shard_map/ppermute | solution.py:18
  53.5 4.0 collective-permute-start.10
  57.5 1.5 collective-permute-start.11
  61.7 1.5 convolution_bitcast_fusion
  92.3 1.5 convolution_add_fusion.7
  96.6 1.7 fusion.5
  111.9 1.8 copy.63
  113.8 2.1 convolution_bitcast_fusion.5
  115.9 4.0 copy.91
  120.0 2.3 convolution_bitcast_fusion.6
  122.3 2.1 convolution_add_fusion.6
  124.7 2.1 convolution_bitcast_fusion.8
  126.8 2.2 convolution_bitcast_fusion.9
  135.9 53.8 %reduce-scatter.3.cloned.1.call-done = f32[27,4,32]{2,0,1:T(8,128)} async-done(((f32[27,64,32]{2,0,1:T(8,128)}), f32[27,4,32]{2,0,1:T(8,128)}) %reduce-scatter.3.cloned.1.call-update) | async-done | bytes 13840 | tf_op jit(solution)/shard_map/reduce_scatter | solution.py:83
  189.8 76.9 %reduce-scatter.5.cloned.1.call-done = f32[27,8,64]{2,0,1:T(8,128)} async-done(((f32[27,128,64]{2,0,1:T(8,128)}), f32[27,8,64]{2,0,1:T(8,128)}) %reduce-scatter.5.cloned.1.call-update) | async-done | bytes 55312 | tf_op jit(solution)/shard_map/reduce_scatter | solution.py:84
  266.7 4.5 %fusion.27 = bf16[1,128,2,8,128]{1,4,3,2,0:T(8,128)(2,1)S(1)} fusion(f32[1,128,2,8,128]{1,4,3,2,0:T(8,128)} %convolution_bitcast_fusion, f32[1,128,2,8,128]{1,4,3,2,0:T(8,128)} %convolution_bitcast_fusion.1, f32[1,128,2,8,128]{1,4,3,2,0:T(8,128)} %convolution_bitcast_fusion.2, f32[1,128,2,8,128]{1,4,3,2,0:T(8,128)} %convolution_bitcast_fusion.3, ...), kind=kOutput, calls=%fused_computation.64 | convolution fusion | flops 36700160 | bytes 12337152 | tf_op jit(solution)/shard_map/oi,bidhw->bodhw/dot_general | solution.py:43
  272.4 136.0 %all-reduce.6.cloned.1.call-done = (f32[27,4,32]{2,0,1:T(8,128)}, f32[27,8,64]{2,0,1:T(8,128)}) async-done(((f32[27,4,32]{2,0,1:T(8,128)}, f32[27,8,64]{2,0,1:T(8,128)}), (f32[27,4,32]{2,0,1:T(8,128)}, f32[27,8,64]{2,0,1:T(8,128)})) %all-reduce.6.cloned.1.call-update) | async-done | bytes 69136 | tf_op jit(solution)/shard_map/psum | solution.py:81
  408.4 1.6 copy.94
  410.0 1.5 copy.93
  (183 shorter events, 76.7 us)
Async XLA Ops:
  7.2 182.6 %reduce-scatter.3.cloned.1.call-start = ((), (), s32[]{:S(2)}) async-start(), calls=%async_computation.2 | async-start | bytes 1114112 | tf_op jit(solution)/shard_map/reduce_scatter | solution.py:83
  8.2 12.1 %copy-start.5 = (bf16[1,32,2,8,128]{4,3,2,1,0:T(8,128)(2,1)S(1)}, bf16[1,32,2,8,128]{4,3,2,1,0:T(8,128)(2,1)}, u32[]{:S(2)}) copy-start(bf16[1,32,2,8,128]{4,3,2,1,0:T(8,128)(2,1)} %param.4) | copy-start | bytes 393220
  8.2 12.1 %collective-permute-start = (bf16[1,32,1,8,128]{4,1,3,2,0:T(8,128)(2,1)S(1)}, bf16[1,32,1,8,128]{4,1,3,2,0:T(8,128)(2,1)S(1)}, u32[]{:S(2)}, u32[]{:S(2)}) collective-permute-start(bf16[1,32,1,8,128]{4,1,3,2,0:T(8,128)(2,1)S(1)} %get-tuple-element.24), channel_id=1, source_target_pairs={{0,4},{4,8},{8,12},{1,5},{5,9},{9,13},{2,6},{6,10},{10,14},{3,7},{... | collective-permute-start | bytes 196616 | tf_op jit(solution)/shard_map/ppermute | solution.py:18
  11.7 11.3 %copy-start.7 = (bf16[27,64,32]{1,2,0:T(8,128)(2,1)S(1)}, bf16[27,64,32]{1,2,0:T(8,128)(2,1)}, u32[]{:S(2)}) copy-start(bf16[27,64,32]{1,2,0:T(8,128)(2,1)} %param.5) | copy-start | bytes 331780
  11.7 8.6 %collective-permute-start.1 = (bf16[1,32,1,8,128]{4,1,3,2,0:T(8,128)(2,1)S(1)}, bf16[1,32,1,8,128]{4,1,3,2,0:T(8,128)(2,1)S(1)}, u32[]{:S(2)}, u32[]{:S(2)}) collective-permute-start(bf16[1,32,1,8,128]{4,1,3,2,0:T(8,128)(2,1)S(1)} %get-tuple-element.23), channel_id=1, source_target_pairs={{4,0},{8,4},{12,8},{5,1},{9,5},{13,9},{6,2},{10,6},{14,10},{7,3},{... | collective-permute-start | bytes 196616 | tf_op jit(solution)/shard_map/ppermute | solution.py:19
  14.4 38.8 %collective-permute-start.8 = (bf16[1,128,1,8,128]{4,1,3,2,0:T(8,128)(2,1)S(1)}, bf16[1,128,1,8,128]{4,1,3,2,0:T(8,128)(2,1)S(1)}, u32[]{:S(2)}, u32[]{:S(2)}) collective-permute-start(bf16[1,128,1,8,128]{4,1,3,2,0:T(8,128)(2,1)S(1)} %get-tuple-element.14), channel_id=1, source_target_pairs={{0,4},{4,8},{8,12},{1,5},{5,9},{9,13},{2,6},{6,10},{10,14},{3,7},{... | collective-permute-start | bytes 786440 | tf_op jit(solution)/shard_map/ppermute | solution.py:18
  19.0 34.5 %collective-permute-start.9 = (bf16[1,128,1,8,128]{4,1,3,2,0:T(8,128)(2,1)S(1)}, bf16[1,128,1,8,128]{4,1,3,2,0:T(8,128)(2,1)S(1)}, u32[]{:S(2)}, u32[]{:S(2)}) collective-permute-start(bf16[1,128,1,8,128]{4,1,3,2,0:T(8,128)(2,1)S(1)} %get-tuple-element.13), channel_id=1, source_target_pairs={{4,0},{8,4},{12,8},{5,1},{9,5},{13,9},{6,2},{10,6},{14,10},{7,3},{... | collective-permute-start | bytes 786440 | tf_op jit(solution)/shard_map/ppermute | solution.py:19
  20.4 2.9 collective-permute-start.2
  21.7 5.6 %collective-permute-start.3 = (bf16[1,32,4,1,128]{4,1,3,2,0:T(8,128)(2,1)S(1)}, bf16[1,32,4,1,128]{4,1,3,2,0:T(8,128)(2,1)S(1)}, u32[]{:S(2)}, u32[]{:S(2)}) collective-permute-start(bf16[1,32,4,1,128]{4,1,3,2,0:T(8,128)(2,1)S(1)} %get-tuple-element.22), channel_id=1, source_target_pairs={{1,0},{2,1},{3,2},{5,4},{6,5},{7,6},{9,8},{10,9},{11,10},{13,12},{... | collective-permute-start | bytes 98312 | tf_op jit(solution)/shard_map/ppermute | solution.py:19
  34.9 6.5 %copy-start = (bf16[1,128,2,8,128]{4,3,2,1,0:T(8,128)(2,1)S(1)}, bf16[1,128,2,8,128]{4,3,2,1,0:T(8,128)(2,1)}, u32[]{:S(2)}) copy-start(bf16[1,128,2,8,128]{4,3,2,1,0:T(8,128)(2,1)} %param.7) | copy-start | bytes 1572868
  34.9 6.5 %copy-start.6 = (bf16[27,128,64]{1,2,0:T(8,128)(2,1)S(1)}, bf16[27,128,64]{1,2,0:T(8,128)(2,1)}, u32[]{:S(2)}) copy-start(bf16[27,128,64]{1,2,0:T(8,128)(2,1)} %param.6) | copy-start | bytes 1327108
  35.5 7.1 %collective-permute-start.4 = (bf16[1,64,1,8,128]{4,1,3,2,0:T(8,128)(2,1)S(1)}, bf16[1,64,1,8,128]{4,1,3,2,0:T(8,128)(2,1)S(1)}, u32[]{:S(2)}, u32[]{:S(2)}) collective-permute-start(bf16[1,64,1,8,128]{4,1,3,2,0:T(8,128)(2,1)S(1)} %get-tuple-element.19), channel_id=1, source_target_pairs={{0,4},{4,8},{8,12},{1,5},{5,9},{9,13},{2,6},{6,10},{10,14},{3,7},{... | collective-permute-start | bytes 393224 | tf_op jit(solution)/shard_map/ppermute | solution.py:18
  40.1 6.9 %collective-permute-start.5 = (bf16[1,64,1,8,128]{4,1,3,2,0:T(8,128)(2,1)S(1)}, bf16[1,64,1,8,128]{4,1,3,2,0:T(8,128)(2,1)S(1)}, u32[]{:S(2)}, u32[]{:S(2)}) collective-permute-start(bf16[1,64,1,8,128]{4,1,3,2,0:T(8,128)(2,1)S(1)} %get-tuple-element.20), channel_id=1, source_target_pairs={{4,0},{8,4},{12,8},{5,1},{9,5},{13,9},{6,2},{10,6},{14,10},{7,3},{... | collective-permute-start | bytes 393224 | tf_op jit(solution)/shard_map/ppermute | solution.py:19
  47.0 12.2 %collective-permute-start.6 = (bf16[1,64,4,1,128]{4,1,3,2,0:T(8,128)(2,1)S(1)}, bf16[1,64,4,1,128]{4,1,3,2,0:T(8,128)(2,1)S(1)}, u32[]{:S(2)}, u32[]{:S(2)}) collective-permute-start(bf16[1,64,4,1,128]{4,1,3,2,0:T(8,128)(2,1)S(1)} %get-tuple-element.17), channel_id=1, source_target_pairs={{0,1},{1,2},{2,3},{4,5},{5,6},{6,7},{8,9},{9,10},{10,11},{12,13},{... | collective-permute-start | bytes 196616 | tf_op jit(solution)/shard_map/ppermute | solution.py:18
  51.6 7.6 %collective-permute-start.7 = (bf16[1,64,4,1,128]{4,1,3,2,0:T(8,128)(2,1)S(1)}, bf16[1,64,4,1,128]{4,1,3,2,0:T(8,128)(2,1)S(1)}, u32[]{:S(2)}, u32[]{:S(2)}) collective-permute-start(bf16[1,64,4,1,128]{4,1,3,2,0:T(8,128)(2,1)S(1)} %get-tuple-element.18), channel_id=1, source_target_pairs={{1,0},{2,1},{3,2},{5,4},{6,5},{7,6},{9,8},{10,9},{11,10},{13,12},{... | collective-permute-start | bytes 196616 | tf_op jit(solution)/shard_map/ppermute | solution.py:19
  53.5 43.1 %collective-permute-start.10 = (bf16[1,128,4,1,128]{4,1,3,2,0:T(8,128)(2,1)S(1)}, bf16[1,128,4,1,128]{4,1,3,2,0:T(8,128)(2,1)S(1)}, u32[]{:S(2)}, u32[]{:S(2)}) collective-permute-start(bf16[1,128,4,1,128]{4,1,3,2,0:T(8,128)(2,1)S(1)} %get-tuple-element.11), channel_id=1, source_target_pairs={{0,1},{1,2},{2,3},{4,5},{5,6},{6,7},{8,9},{9,10},{10,11},{12,13},{... | collective-permute-start | bytes 393224 | tf_op jit(solution)/shard_map/ppermute | solution.py:18
  57.5 39.1 %collective-permute-start.11 = (bf16[1,128,4,1,128]{4,1,3,2,0:T(8,128)(2,1)S(1)}, bf16[1,128,4,1,128]{4,1,3,2,0:T(8,128)(2,1)S(1)}, u32[]{:S(2)}, u32[]{:S(2)}) collective-permute-start(bf16[1,128,4,1,128]{4,1,3,2,0:T(8,128)(2,1)S(1)} %get-tuple-element.12), channel_id=1, source_target_pairs={{1,0},{2,1},{3,2},{5,4},{6,5},{7,6},{9,8},{10,9},{11,10},{13,12},{... | collective-permute-start | bytes 393224 | tf_op jit(solution)/shard_map/ppermute | solution.py:19
  63.3 26.8 %copy-start.4 = (bf16[1,64,4,9,128]{4,1,3,2,0:T(8,128)(2,1)}, bf16[1,64,4,9,128]{4,1,3,2,0:T(8,128)(2,1)S(1)}, u32[]{:S(2)}) copy-start(bf16[1,64,4,9,128]{4,1,3,2,0:T(8,128)(2,1)S(1)} %get-tuple-element.15) | copy-start | bytes 1769476
  63.3 28.7 %copy-start.3 = (bf16[1,64,4,9,128]{4,1,3,2,0:T(8,128)(2,1)}, bf16[1,64,4,9,128]{4,1,3,2,0:T(8,128)(2,1)S(1)}, u32[]{:S(2)}) copy-start(bf16[1,64,4,9,128]{4,1,3,2,0:T(8,128)(2,1)S(1)} %get-tuple-element.16) | copy-start | bytes 1769476
  113.8 152.9 %reduce-scatter.5.cloned.1.call-start = ((), (), s32[]{:S(2)}) async-start(), calls=%async_computation.3 | async-start | bytes 2228224 | tf_op jit(solution)/shard_map/reduce_scatter | solution.py:84
  120.0 2.3 copy-start.1
  124.4 284.0 %all-reduce.6.cloned.1.call-start = ((), (), s32[]{:S(2)}) async-start(), calls=%async_computation.4 | async-start | bytes 393216 | tf_op jit(solution)/shard_map/psum | solution.py:81
  124.7 4.3 %copy-start.2 = (f32[2,8,128,128]{3,2,1,0:T(8,128)S(1)}, f32[2,8,128,128]{3,2,1,0:T(8,128)}, u32[]{:S(2)}) copy-start(f32[2,8,128,128]{3,2,1,0:T(8,128)} %convolution_add_fusion.6) | copy-start | bytes 3145732
Sparse Core Ops, SparseCore 0:
  113.9 75.8 reduce-scatter.2
  192.5 74.1 reduce-scatter.4
  269.6 138.7 all-reduce.5
where the time goes:
time: 419 us; the launch traced here: 418 us
  waiting for transfers between devices  276 us (66%)
  matrix products  80.8 us (19%)
  starting transfers between devices  31 us (7%)
  between operations  14.5 us (3%)
  local copies, waits for them, and re-layouts  12.7 us (3%)
    psum x1, waiting for transfers between devices, per_device(): summed = lax.psum((grad_first, grad_second), ('dep', 'hgt'))  136 us
    reduce_scatter x1, waiting for transfers between devices, per_device(): lax.psum_scatter(summed[1], 'dp', scatter_dimension=1, tiled=True)  76.9 us
    reduce_scatter x1, waiting for transfers between devices, per_device(): lax.psum_scatter(summed[0], 'dp', scatter_dimension=1, tiled=True)  53.8 us
    dot_general x54, matrix products, convolve(): jnp.einsum('oi,bidhw->bodhw', kernel[number], piece, preferred_element_ty...  41.9 us
    dot_general x54, matrix products, kernel_grad(): jnp.einsum('bodhw,bidhw->oi', upstream, piece, preferred_element_type=jnp...  31.1 us
    ppermute x6, starting transfers between devices, extended_2(): before = lax.ppermute(last, axis, up)  22.5 us
    ppermute x6, waiting for transfers between devices, extended_2(): after = lax.ppermute(leading, axis, down)  8.42 us
  transfers between devices with their start and end apart: 15, of which 6 were waited for; matrix products, arithmetic and copies ran while one was open for 18% of the time, Pallas kernels for 0%

commit v1 on v0

--- a/solution.py
+++ b/solution.py
@@ -78,7 +78,7 @@
     sigma = jax.nn.sigmoid(pre)
     delta = (back * (sigma * (1.0 + pre * (1.0 - sigma)))).astype(jnp.bfloat16)
     grad_first = kernel_grad(delta, vol_rim, depth, height, width)
-    summed = lax.psum((grad_first, grad_second), ("dep", "hgt"))
+    summed = lax.psum(lax.psum((grad_first, grad_second), "dep"), "hgt")
     grad_first, grad_second = (
         lax.psum_scatter(summed[0], "dp", scatter_dimension=1, tiled=True),
         lax.psum_scatter(summed[1], "dp", scatter_dimension=1, tiled=True),

time: 419 us -> 377 us (0.90)
  waiting for transfers between devices: 276 us -> 230 us
    psum x1 -> x2, waiting for transfers between devices: 136 us -> 90.2 us  [per_device(): summed = lax.psum(lax.psum((grad_first, grad_second), 'dep'), 'hgt')]
  transfers between devices with their start and end apart: 15 -> 16, of which waited for: 6 -> 7; matrix products, arithmetic and copies ran while one was open for 18% -> 20% of each run, Pallas kernels for 0% -> 0%
where the time goes in v1:
time: 377 us; the launch traced here: 373 us
  waiting for transfers between devices  230 us (61%)
  matrix products  81.6 us (22%)
  starting transfers between devices  31 us (8%)
  between operations  14.5 us (4%)
  local copies, waits for them, and re-layouts  12.7 us (3%)
    psum x2, waiting for transfers between devices, per_device(): summed = lax.psum(lax.psum((grad_first, grad_second), 'dep'), 'hgt')  90.2 us
    reduce_scatter x1, waiting for transfers between devices, per_device(): lax.psum_scatter(summed[1], 'dp', scatter_dimension=1, tiled=True)  76.8 us
    reduce_scatter x1, waiting for transfers between devices, per_device(): lax.psum_scatter(summed[0], 'dp', scatter_dimension=1, tiled=True)  53.9 us
    dot_general x54, matrix products, convolve(): jnp.einsum('oi,bidhw->bodhw', kernel[number], piece, preferred_element_ty...  42.6 us
    dot_general x54, matrix products, kernel_grad(): jnp.einsum('bodhw,bidhw->oi', upstream, piece, preferred_element_type=jnp...  31.1 us
    ppermute x6, starting transfers between devices, extended_2(): before = lax.ppermute(last, axis, up)  22.5 us
    ppermute x6, waiting for transfers between devices, extended_2(): after = lax.ppermute(leading, axis, down)  8.42 us
    ppermute x6, starting transfers between devices, extended_2(): after = lax.ppermute(leading, axis, down)  8.06 us
  transfers between devices with their start and end apart: 16, of which 7 were waited for; matrix products, arithmetic and copies ran while one was open for 20% of the time, Pallas kernels for 0%

profile of v1, /device:TPU:8, one launch (start us, length us, event | category | flops | bytes accessed | tf_op | source)
XLA Modules:
  0.0 373.1 jit_solution(13437642956782821404)
XLA Ops:
  8.2 3.5 collective-permute-start
  14.4 4.6 %collective-permute-start.8 = (bf16[1,128,1,8,128]{4,1,3,2,0:T(8,128)(2,1)S(1)}, bf16[1,128,1,8,128]{4,1,3,2,0:T(8,128)(2,1)S(1)}, u32[]{:S(2)}, u32[]{:S(2)}) collective-permute-start(bf16[1,128,1,8,128]{4,1,3,2,0:T(8,128)(2,1)S(1)} %get-tuple-element.16), channel_id=1, source_target_pairs={{0,4},{4,8},{8,12},{1,5},{5,9},{9,13},{2,6},{6,10},{10,14},{3,7},{... | collective-permute-start | bytes 786440 | tf_op jit(solution)/shard_map/ppermute | solution.py:18
  23.3 4.0 %collective-permute-done.3 = bf16[1,32,4,1,128]{4,1,3,2,0:T(8,128)(2,1)S(1)} collective-permute-done((bf16[1,32,4,1,128]{4,1,3,2,0:T(8,128)(2,1)S(1)}, bf16[1,32,4,1,128]{4,1,3,2,0:T(8,128)(2,1)S(1)}, u32[]{:S(2)}, u32[]{:S(2)}) %collective-permute-start.3) | collective-permute-done | bytes 32800 | tf_op jit(solution)/shard_map/ppermute | solution.py:19
  35.5 4.6 %collective-permute-start.4 = (bf16[1,64,1,8,128]{4,1,3,2,0:T(8,128)(2,1)S(1)}, bf16[1,64,1,8,128]{4,1,3,2,0:T(8,128)(2,1)S(1)}, u32[]{:S(2)}, u32[]{:S(2)}) collective-permute-start(bf16[1,64,1,8,128]{4,1,3,2,0:T(8,128)(2,1)S(1)} %get-tuple-element.21), channel_id=1, source_target_pairs={{0,4},{4,8},{8,12},{1,5},{5,9},{9,13},{2,6},{6,10},{10,14},{3,7},{... | collective-permute-start | bytes 393224 | tf_op jit(solution)/shard_map/ppermute | solution.py:18
  42.6 4.4 %collective-permute-done.5 = bf16[1,64,1,8,128]{4,1,3,2,0:T(8,128)(2,1)S(1)} collective-permute-done((bf16[1,64,1,8,128]{4,1,3,2,0:T(8,128)(2,1)S(1)}, bf16[1,64,1,8,128]{4,1,3,2,0:T(8,128)(2,1)S(1)}, u32[]{:S(2)}, u32[]{:S(2)}) %collective-permute-start.5) | collective-permute-done | bytes 131104 | tf_op jit(solution)/shard_map/ppermute | solution.py:19
  47.0 4.6 %collective-permute-start.6 = (bf16[1,64,4,1,128]{4,1,3,2,0:T(8,128)(2,1)S(1)}, bf16[1,64,4,1,128]{4,1,3,2,0:T(8,128)(2,1)S(1)}, u32[]{:S(2)}, u32[]{:S(2)}) collective-permute-start(bf16[1,64,4,1,128]{4,1,3,2,0:T(8,128)(2,1)S(1)} %get-tuple-element.19), channel_id=1, source_target_pairs={{0,1},{1,2},{2,3},{4,5},{5,6},{6,7},{8,9},{9,10},{10,11},{12,13},{... | collective-permute-start | bytes 196616 | tf_op jit(solution)/shard_map/ppermute | solution.py:18
  53.5 4.0 %collective-permute-start.10 = (bf16[1,128,4,1,128]{4,1,3,2,0:T(8,128)(2,1)S(1)}, bf16[1,128,4,1,128]{4,1,3,2,0:T(8,128)(2,1)S(1)}, u32[]{:S(2)}, u32[]{:S(2)}) collective-permute-start(bf16[1,128,4,1,128]{4,1,3,2,0:T(8,128)(2,1)S(1)} %get-tuple-element.13), channel_id=1, source_target_pairs={{0,1},{1,2},{2,3},{4,5},{5,6},{6,7},{8,9},{9,10},{10,11},{12,13},{... | collective-permute-start | bytes 393224 | tf_op jit(solution)/shard_map/ppermute | solution.py:18
  90.9 1.5 convolution_add_fusion.7
  92.4 1.5 convolution_bitcast_fusion
  95.2 1.7 fusion.5
  110.6 1.8 copy.63
  112.5 2.2 convolution_bitcast_fusion.3
  114.6 4.0 %copy.91 = f32[27,128,64]{2,0,1:T(8,128)} copy(f32[27,128,64]{1,2,0:T(8,128)} %fusion.59) | data formatting | bytes 1769472 | tf_op jit(solution)/shard_map/stack | solution.py:58
  118.6 2.2 convolution_bitcast_fusion.5
  120.8 2.1 convolution_add_fusion.6
  123.3 2.3 convolution_bitcast_fusion.6
  125.6 2.0 convolution_bitcast_fusion.8
  134.5 53.9 %reduce-scatter.3.cloned.1.call-done = f32[27,4,32]{2,0,1:T(8,128)} async-done(((f32[27,64,32]{2,0,1:T(8,128)}), f32[27,4,32]{2,0,1:T(8,128)}) %reduce-scatter.3.cloned.1.call-update) | async-done | bytes 13840 | tf_op jit(solution)/shard_map/reduce_scatter | solution.py:83
  188.4 76.8 %reduce-scatter.5.cloned.1.call-done = f32[27,8,64]{2,0,1:T(8,128)} async-done(((f32[27,128,64]{2,0,1:T(8,128)}), f32[27,8,64]{2,0,1:T(8,128)}) %reduce-scatter.5.cloned.1.call-update) | async-done | bytes 55312 | tf_op jit(solution)/shard_map/reduce_scatter | solution.py:84
  265.4 2.2 convolution_bitcast_fusion.9
  267.5 48.3 %all-reduce.10.cloned.1.call-done = (f32[27,4,32]{2,0,1:T(8,128)}, f32[27,8,64]{2,0,1:T(8,128)}) async-done(((f32[27,4,32]{2,0,1:T(8,128)}, f32[27,8,64]{2,0,1:T(8,128)}), (f32[27,4,32]{2,0,1:T(8,128)}, f32[27,8,64]{2,0,1:T(8,128)})) %all-reduce.10.cloned.1.call-update) | async-done | bytes 69136 | tf_op jit(solution)/shard_map/psum | solution.py:81
  315.9 4.5 %fusion.27 = bf16[1,128,2,8,128]{1,4,3,2,0:T(8,128)(2,1)S(1)} fusion(f32[1,128,2,8,128]{1,4,3,2,0:T(8,128)} %convolution_bitcast_fusion, f32[1,128,2,8,128]{1,4,3,2,0:T(8,128)} %convolution_bitcast_fusion.1, f32[1,128,2,8,128]{1,4,3,2,0:T(8,128)} %convolution_bitcast_fusion.2, f32[1,128,2,8,128]{1,4,3,2,0:T(8,128)} %convolution_bitcast_fusion.3, ...), kind=kOutput, calls=%fused_computation.64 | convolution fusion | flops 36700160 | bytes 12337152 | tf_op jit(solution)/shard_map/oi,bidhw->bodhw/dot_general | solution.py:43
  321.6 41.9 %all-reduce.8.cloned.1.call-done = (f32[27,4,32]{2,0,1:T(8,128)}, f32[27,8,64]{2,0,1:T(8,128)}) async-done(((f32[27,4,32]{2,0,1:T(8,128)}, f32[27,8,64]{2,0,1:T(8,128)}), (f32[27,4,32]{2,0,1:T(8,128)}, f32[27,8,64]{2,0,1:T(8,128)})) %all-reduce.8.cloned.1.call-update) | async-done | bytes 69136 | tf_op jit(solution)/shard_map/psum | solution.py:81
  363.5 1.6 copy.94
  (186 shorter events, 78.4 us)
Async XLA Ops:
  7.2 181.3 %reduce-scatter.3.cloned.1.call-start = ((), (), s32[]{:S(2)}) async-start(), calls=%async_computation.2 | async-start | bytes 1114112 | tf_op jit(solution)/shard_map/reduce_scatter | solution.py:83
  8.2 12.1 %copy-start.5 = (bf16[1,32,2,8,128]{4,3,2,1,0:T(8,128)(2,1)S(1)}, bf16[1,32,2,8,128]{4,3,2,1,0:T(8,128)(2,1)}, u32[]{:S(2)}) copy-start(bf16[1,32,2,8,128]{4,3,2,1,0:T(8,128)(2,1)} %param.4) | copy-start | bytes 393220
  8.2 12.1 %collective-permute-start = (bf16[1,32,1,8,128]{4,1,3,2,0:T(8,128)(2,1)S(1)}, bf16[1,32,1,8,128]{4,1,3,2,0:T(8,128)(2,1)S(1)}, u32[]{:S(2)}, u32[]{:S(2)}) collective-permute-start(bf16[1,32,1,8,128]{4,1,3,2,0:T(8,128)(2,1)S(1)} %get-tuple-element.26), channel_id=1, source_target_pairs={{0,4},{4,8},{8,12},{1,5},{5,9},{9,13},{2,6},{6,10},{10,14},{3,7},{... | collective-permute-start | bytes 196616 | tf_op jit(solution)/shard_map/ppermute | solution.py:18
  11.7 11.3 %copy-start.7 = (bf16[27,64,32]{1,2,0:T(8,128)(2,1)S(1)}, bf16[27,64,32]{1,2,0:T(8,128)(2,1)}, u32[]{:S(2)}) copy-start(bf16[27,64,32]{1,2,0:T(8,128)(2,1)} %param.5) | copy-start | bytes 331780
  11.7 8.6 %collective-permute-start.1 = (bf16[1,32,1,8,128]{4,1,3,2,0:T(8,128)(2,1)S(1)}, bf16[1,32,1,8,128]{4,1,3,2,0:T(8,128)(2,1)S(1)}, u32[]{:S(2)}, u32[]{:S(2)}) collective-permute-start(bf16[1,32,1,8,128]{4,1,3,2,0:T(8,128)(2,1)S(1)} %get-tuple-element.25), channel_id=1, source_target_pairs={{4,0},{8,4},{12,8},{5,1},{9,5},{13,9},{6,2},{10,6},{14,10},{7,3},{... | collective-permute-start | bytes 196616 | tf_op jit(solution)/shard_map/ppermute | solution.py:19
  14.4 38.8 %collective-permute-start.8 = (bf16[1,128,1,8,128]{4,1,3,2,0:T(8,128)(2,1)S(1)}, bf16[1,128,1,8,128]{4,1,3,2,0:T(8,128)(2,1)S(1)}, u32[]{:S(2)}, u32[]{:S(2)}) collective-permute-start(bf16[1,128,1,8,128]{4,1,3,2,0:T(8,128)(2,1)S(1)} %get-tuple-element.16), channel_id=1, source_target_pairs={{0,4},{4,8},{8,12},{1,5},{5,9},{9,13},{2,6},{6,10},{10,14},{3,7},{... | collective-permute-start | bytes 786440 | tf_op jit(solution)/shard_map/ppermute | solution.py:18
  19.0 34.5 %collective-permute-start.9 = (bf16[1,128,1,8,128]{4,1,3,2,0:T(8,128)(2,1)S(1)}, bf16[1,128,1,8,128]{4,1,3,2,0:T(8,128)(2,1)S(1)}, u32[]{:S(2)}, u32[]{:S(2)}) collective-permute-start(bf16[1,128,1,8,128]{4,1,3,2,0:T(8,128)(2,1)S(1)} %get-tuple-element.15), channel_id=1, source_target_pairs={{4,0},{8,4},{12,8},{5,1},{9,5},{13,9},{6,2},{10,6},{14,10},{7,3},{... | collective-permute-start | bytes 786440 | tf_op jit(solution)/shard_map/ppermute | solution.py:19
  20.4 2.9 collective-permute-start.2
  21.7 5.6 %collective-permute-start.3 = (bf16[1,32,4,1,128]{4,1,3,2,0:T(8,128)(2,1)S(1)}, bf16[1,32,4,1,128]{4,1,3,2,0:T(8,128)(2,1)S(1)}, u32[]{:S(2)}, u32[]{:S(2)}) collective-permute-start(bf16[1,32,4,1,128]{4,1,3,2,0:T(8,128)(2,1)S(1)} %get-tuple-element.24), channel_id=1, source_target_pairs={{1,0},{2,1},{3,2},{5,4},{6,5},{7,6},{9,8},{10,9},{11,10},{13,12},{... | collective-permute-start | bytes 98312 | tf_op jit(solution)/shard_map/ppermute | solution.py:19
  34.9 6.5 %copy-start = (bf16[1,128,2,8,128]{4,3,2,1,0:T(8,128)(2,1)S(1)}, bf16[1,128,2,8,128]{4,3,2,1,0:T(8,128)(2,1)}, u32[]{:S(2)}) copy-start(bf16[1,128,2,8,128]{4,3,2,1,0:T(8,128)(2,1)} %param.7) | copy-start | bytes 1572868
  34.9 6.5 %copy-start.6 = (bf16[27,128,64]{1,2,0:T(8,128)(2,1)S(1)}, bf16[27,128,64]{1,2,0:T(8,128)(2,1)}, u32[]{:S(2)}) copy-start(bf16[27,128,64]{1,2,0:T(8,128)(2,1)} %param.6) | copy-start | bytes 1327108
  35.5 7.1 %collective-permute-start.4 = (bf16[1,64,1,8,128]{4,1,3,2,0:T(8,128)(2,1)S(1)}, bf16[1,64,1,8,128]{4,1,3,2,0:T(8,128)(2,1)S(1)}, u32[]{:S(2)}, u32[]{:S(2)}) collective-permute-start(bf16[1,64,1,8,128]{4,1,3,2,0:T(8,128)(2,1)S(1)} %get-tuple-element.21), channel_id=1, source_target_pairs={{0,4},{4,8},{8,12},{1,5},{5,9},{9,13},{2,6},{6,10},{10,14},{3,7},{... | collective-permute-start | bytes 393224 | tf_op jit(solution)/shard_map/ppermute | solution.py:18
  40.1 6.9 %collective-permute-start.5 = (bf16[1,64,1,8,128]{4,1,3,2,0:T(8,128)(2,1)S(1)}, bf16[1,64,1,8,128]{4,1,3,2,0:T(8,128)(2,1)S(1)}, u32[]{:S(2)}, u32[]{:S(2)}) collective-permute-start(bf16[1,64,1,8,128]{4,1,3,2,0:T(8,128)(2,1)S(1)} %get-tuple-element.22), channel_id=1, source_target_pairs={{4,0},{8,4},{12,8},{5,1},{9,5},{13,9},{6,2},{10,6},{14,10},{7,3},{... | collective-permute-start | bytes 393224 | tf_op jit(solution)/shard_map/ppermute | solution.py:19
  47.0 12.2 %collective-permute-start.6 = (bf16[1,64,4,1,128]{4,1,3,2,0:T(8,128)(2,1)S(1)}, bf16[1,64,4,1,128]{4,1,3,2,0:T(8,128)(2,1)S(1)}, u32[]{:S(2)}, u32[]{:S(2)}) collective-permute-start(bf16[1,64,4,1,128]{4,1,3,2,0:T(8,128)(2,1)S(1)} %get-tuple-element.19), channel_id=1, source_target_pairs={{0,1},{1,2},{2,3},{4,5},{5,6},{6,7},{8,9},{9,10},{10,11},{12,13},{... | collective-permute-start | bytes 196616 | tf_op jit(solution)/shard_map/ppermute | solution.py:18
  51.6 7.6 %collective-permute-start.7 = (bf16[1,64,4,1,128]{4,1,3,2,0:T(8,128)(2,1)S(1)}, bf16[1,64,4,1,128]{4,1,3,2,0:T(8,128)(2,1)S(1)}, u32[]{:S(2)}, u32[]{:S(2)}) collective-permute-start(bf16[1,64,4,1,128]{4,1,3,2,0:T(8,128)(2,1)S(1)} %get-tuple-element.20), channel_id=1, source_target_pairs={{1,0},{2,1},{3,2},{5,4},{6,5},{7,6},{9,8},{10,9},{11,10},{13,12},{... | collective-permute-start | bytes 196616 | tf_op jit(solution)/shard_map/ppermute | solution.py:19
  53.5 41.7 %collective-permute-start.10 = (bf16[1,128,4,1,128]{4,1,3,2,0:T(8,128)(2,1)S(1)}, bf16[1,128,4,1,128]{4,1,3,2,0:T(8,128)(2,1)S(1)}, u32[]{:S(2)}, u32[]{:S(2)}) collective-permute-start(bf16[1,128,4,1,128]{4,1,3,2,0:T(8,128)(2,1)S(1)} %get-tuple-element.13), channel_id=1, source_target_pairs={{0,1},{1,2},{2,3},{4,5},{5,6},{6,7},{8,9},{9,10},{10,11},{12,13},{... | collective-permute-start | bytes 393224 | tf_op jit(solution)/shard_map/ppermute | solution.py:18
  57.5 37.7 %collective-permute-start.11 = (bf16[1,128,4,1,128]{4,1,3,2,0:T(8,128)(2,1)S(1)}, bf16[1,128,4,1,128]{4,1,3,2,0:T(8,128)(2,1)S(1)}, u32[]{:S(2)}, u32[]{:S(2)}) collective-permute-start(bf16[1,128,4,1,128]{4,1,3,2,0:T(8,128)(2,1)S(1)} %get-tuple-element.14), channel_id=1, source_target_pairs={{1,0},{2,1},{3,2},{5,4},{6,5},{7,6},{9,8},{10,9},{11,10},{13,12},{... | collective-permute-start | bytes 393224 | tf_op jit(solution)/shard_map/ppermute | solution.py:19
  61.9 26.8 %copy-start.4 = (bf16[1,64,4,9,128]{4,1,3,2,0:T(8,128)(2,1)}, bf16[1,64,4,9,128]{4,1,3,2,0:T(8,128)(2,1)S(1)}, u32[]{:S(2)}) copy-start(bf16[1,64,4,9,128]{4,1,3,2,0:T(8,128)(2,1)S(1)} %get-tuple-element.17) | copy-start | bytes 1769476
  61.9 28.7 %copy-start.3 = (bf16[1,64,4,9,128]{4,1,3,2,0:T(8,128)(2,1)}, bf16[1,64,4,9,128]{4,1,3,2,0:T(8,128)(2,1)S(1)}, u32[]{:S(2)}) copy-start(bf16[1,64,4,9,128]{4,1,3,2,0:T(8,128)(2,1)S(1)} %get-tuple-element.18) | copy-start | bytes 1769476
  112.4 152.9 %reduce-scatter.5.cloned.1.call-start = ((), (), s32[]{:S(2)}) async-start(), calls=%async_computation.3 | async-start | bytes 2228224 | tf_op jit(solution)/shard_map/reduce_scatter | solution.py:84
  118.6 2.2 copy-start.1
  122.9 192.9 %all-reduce.10.cloned.1.call-start = ((), (), s32[]{:S(2)}) async-start(), calls=%async_computation.5 | async-start | bytes 393216 | tf_op jit(solution)/shard_map/psum | solution.py:81
  123.2 4.4 %copy-start.2 = (f32[2,8,128,128]{3,2,1,0:T(8,128)S(1)}, f32[2,8,128,128]{3,2,1,0:T(8,128)}, u32[]{:S(2)}) copy-start(f32[2,8,128,128]{3,2,1,0:T(8,128)} %convolution_add_fusion.6) | copy-start | bytes 3145732
  265.3 98.2 %all-reduce.8.cloned.1.call-start = ((), (), s32[]{:S(2)}) async-start(), calls=%async_computation.4 | async-start | bytes 393216 | tf_op jit(solution)/shard_map/psum | solution.py:81
Sparse Core Ops, SparseCore 0:
  112.5 75.8 reduce-scatter.2
  191.1 74.1 reduce-scatter.4
  267.8 48.0 all-reduce.9
  318.4 45.0 all-reduce.7
